TPU v7x, 32 devices: a whole 2x2x4 slice. The times are simulated.
32 devices in a mesh: aa: 4 (over z), ba: 8 (over y, x, core).
Axes of the slice: x: 2, y: 2, z: 4, core: 2. Of those that a mesh axis runs over, the one named last changes fastest.
Arguments:
- feats: bfloat16 [4, 32, 128, 256], P('aa', 'ba'), may hold values from -6 to 6
- conv_one: bfloat16 [3, 3, 3, 256, 256], replicated, may hold values from -0.078125 to 0.078125
- bias_one: float32 [256], replicated, may hold values from -3 to 3
- conv_two: bfloat16 [3, 3, 3, 256, 256], replicated, may hold values from -0.078125 to 0.078125
- bias_two: float32 [256], replicated, may hold values from -3 to 3
- patch_weight: bfloat16 [2, 2, 256, 128], replicated, may hold values from -0.1875 to 0.1875
- patch_bias: float32 [128], replicated, may hold values from -3 to 3
- embed_weight: bfloat16 [128, 2048], replicated, may hold values from -0.5 to 0.5
- embed_bias: float32 [2048], replicated, may hold values from -6 to 6
- norm_gain: float32 [2048], replicated, may hold values from 0.1 to 1.9
- w_query: bfloat16 [2048, 2048], P(None, 'ba'), may hold values from -2 to 2
- w_key: bfloat16 [2048, 2048], P(None, 'ba'), may hold values from -2 to 2
- w_value: bfloat16 [2048, 2048], P(None, 'ba'), may hold values from -0.125 to 0.125
- w_velocity: bfloat16 [2048, 128], P('ba'), may hold values from -0.5 to 0.5
Outputs:
- velocity: float32 [4096, 128], P(('aa', 'ba'))
All inputs are finite; a program needn't handle non-finite values.
Results may differ from a plain program's by a relative error of at most 0.035.
Values may be sent and summed in bfloat16 or wider, within the bound.
A program may use at most 128 MiB of HBM per device.

v0:
```python
import math
import jax
import jax.numpy as jnp
from jax import lax
from jax.sharding import PartitionSpec as P

HEAD_DIM = 64


def with_halo(cells, sides, width):
    for axis, dim in sides:
        count = lax.axis_size(axis)
        ends = count - 1
        head = lax.slice_in_dim(cells, 0, width, axis=dim)
        tail = lax.slice_in_dim(cells, cells.shape[dim] - width, cells.shape[dim], axis=dim)
        cells = jnp.concatenate(
            [
                lax.ppermute(tail, axis, [(i, (i + 1) % count) for i in range(ends)]),
                cells,
                lax.ppermute(head, axis, [((i + 1) % count, i) for i in range(ends)]),
            ],
            axis=dim,
        )
    return cells


def convolve(field, kernel, bias):
    frames, rows, width, chans = field.shape
    padded = with_halo(field, (("aa", 0), ("ba", 1)), 1)
    padded = jnp.pad(padded, ((0, 0), (0, 0), (1, 1), (0, 0)))
    total = jnp.zeros((frames * rows * width, kernel.shape[-1]), jnp.float32)
    for shift_t in range(3):
        for shift_r in range(3):
            window = padded[shift_t : shift_t + frames, shift_r : shift_r + rows]
            stacked = jnp.concatenate(
                [window[:, :, shift_w : shift_w + width] for shift_w in range(3)], axis=-1
            )
            total = total + jnp.dot(
                stacked.reshape(-1, 3 * chans),
                kernel[shift_t, shift_r].reshape(3 * chans, -1),
                preferred_element_type=jnp.float32,
            )
    return (total + bias).reshape(frames, rows, width, -1)


def patchify(field, weight, bias):
    frames, rows, width, chans = field.shape
    blocks = (
        field.reshape(frames, rows // 2, 2, width // 2, 2, chans)
        .transpose(0, 1, 3, 2, 4, 5)
        .reshape(-1, 4 * chans)
    )
    return (
        jnp.dot(blocks, weight.reshape(4 * chans, -1), preferred_element_type=jnp.float32) + bias
    ).astype(jnp.bfloat16)


def normalize(latent_rows, embed_weight, embed_bias, norm_gain):
    hidden = jnp.dot(latent_rows, embed_weight, preferred_element_type=jnp.float32) + embed_bias
    center = hidden - hidden.mean(-1, keepdims=True)
    spread = (center * center).mean(-1, keepdims=True)
    return (center * lax.rsqrt(spread + 1e-05) * norm_gain).astype(jnp.bfloat16)


def attend(queries, keys, values):
    rows, width = queries.shape
    heads = width // HEAD_DIM
    scale = HEAD_DIM ** (-0.5)
    query_heads = queries.reshape(rows, heads, HEAD_DIM)
    start_state = (
        jnp.full((heads, rows), -jnp.inf, jnp.float32),
        jnp.zeros((heads, rows), jnp.float32),
        jnp.zeros((rows, heads, HEAD_DIM), jnp.float32),
    )
    key_rows = lax.all_gather(keys, "aa", axis=0, tiled=True)
    value_rows = lax.all_gather(values, "aa", axis=0, tiled=True)
    count = key_rows.shape[0]
    block = math.gcd(count, 1024)

    def one_step(index, state):
        best, denom, accum = state
        key_block = lax.dynamic_slice_in_dim(key_rows, index * block, block, 0).reshape(
            block, heads, HEAD_DIM
        )
        value_block = lax.dynamic_slice_in_dim(value_rows, index * block, block, 0).reshape(
            block, heads, HEAD_DIM
        )
        scores = (
            jnp.einsum("qhd,khd->hqk", query_heads, key_block, preferred_element_type=jnp.float32)
            * scale
        )
        peak = jnp.maximum(best, scores.max(-1))
        probs = jnp.exp(scores - peak[..., None])
        fade = jnp.exp(best - peak)
        denom = denom * fade + probs.sum(-1)
        accum = accum * fade.T[..., None] + jnp.einsum(
            "hqk,khd->qhd",
            probs.astype(jnp.bfloat16),
            value_block,
            preferred_element_type=jnp.float32,
        )
        return (peak, denom, accum)

    best, denom, accum = lax.fori_loop(0, count // block, one_step, start_state)
    return (accum / denom.T[..., None]).reshape(rows, width).astype(jnp.bfloat16)


def on_device(
    feats,
    conv_one,
    bias_one,
    conv_two,
    bias_two,
    patch_weight,
    patch_bias,
    embed_weight,
    embed_bias,
    norm_gain,
    w_query,
    w_key,
    w_value,
    w_velocity,
):
    first = jax.nn.gelu(convolve(feats, conv_one, bias_one), approximate=False).astype(jnp.bfloat16)
    second = (
        first.astype(jnp.float32)
        + jax.nn.gelu(convolve(first, conv_two, bias_two), approximate=False)
    ).astype(jnp.bfloat16)
    latents = patchify(second, patch_weight, patch_bias)
    width = w_query.shape[1]
    w_joined = jnp.concatenate([w_query, w_key, w_value], axis=1)
    joined = jnp.dot(
        normalize(
            lax.all_gather(latents, "ba", axis=0, tiled=True), embed_weight, embed_bias, norm_gain
        ),
        w_joined,
        preferred_element_type=jnp.float32,
    ).astype(jnp.bfloat16)
    attended = attend(joined[:, :width], joined[:, width : 2 * width], joined[:, 2 * width :])
    return lax.psum_scatter(
        jnp.dot(attended, w_velocity, preferred_element_type=jnp.float32).astype(jnp.bfloat16),
        "ba",
        scatter_dimension=0,
        tiled=True,
    ).astype(jnp.float32)


def solution(mesh):
    return jax.shard_map(
        on_device,
        mesh=mesh,
        in_specs=(
            P("aa", "ba", None, None),
            P(),
            P(),
            P(),
            P(),
            P(),
            P(),
            P(),
            P(),
            P(),
            P(None, "ba"),
            P(None, "ba"),
            P(None, "ba"),
            P("ba", None),
        ),
        out_specs=P(("aa", "ba"), None),
        check_vma=False,
    )
```

profile of v0, /device:TPU:0, one launch (start us, length us, event | category | flops | bytes accessed | tf_op | source)
XLA Modules:
  0.0 332.6 jit_solution(549942878547130094)
XLA Ops:
  6.5 5.1 %collective-permute-start = (bf16[1,4,128,256]{3,2,1,0:T(8,128)(2,1)}, bf16[1,4,128,256]{3,2,1,0:T(8,128)(2,1)S(1)}, u32[]{:S(2)}, u32[]{:S(2)}) collective-permute-start(bf16[1,4,128,256]{3,2,1,0:T(8,128)(2,1)} %param.16), channel_id=1, source_target_pairs={{0,8},{8,16},{16,24},{1,9},{9,17},{17,25},{2,10},{10,18},{18,26},{... | collective-permute-start | bytes 786440 | tf_op jit(solution)/shard_map/ppermute | solution.py:18
  11.6 1.3 collective-permute-start.1
  12.9 4.5 %collective-permute-done = bf16[1,4,128,256]{3,2,1,0:T(8,128)(2,1)S(1)} collective-permute-done((bf16[1,4,128,256]{3,2,1,0:T(8,128)(2,1)}, bf16[1,4,128,256]{3,2,1,0:T(8,128)(2,1)S(1)}, u32[]{:S(2)}, u32[]{:S(2)}) %collective-permute-start) | collective-permute-done | bytes 262176 | tf_op jit(solution)/shard_map/ppermute | solution.py:18
  17.5 1.0 constant_dynamic-update-slice_fusion.1
  18.5 3.0 collective-permute-done.1
  21.6 1.3 collective-permute-start.2
  22.9 1.3 collective-permute-start.3
  24.2 2.2 fusion.102
  26.4 1.6 collective-permute-done.3
  27.9 0.6 select_maximum_fusion.5
  28.5 0.9 fusion.105
  30.6 0.4 convolution_add_fusion.15
  32.5 0.4 convolution_add_fusion.10
  33.6 2.1 fusion.69
  35.7 1.1 fusion.66
  36.8 3.5 %collective-permute-start.4 = (bf16[1,4,128,256]{3,2,1,0:T(8,128)(2,1)S(1)}, bf16[1,4,128,256]{3,2,1,0:T(8,128)(2,1)S(1)}, u32[]{:S(2)}, u32[]{:S(2)}) collective-permute-start(bf16[1,4,128,256]{3,2,1,0:T(8,128)(2,1)S(1)} %fusion.66), channel_id=1, source_target_pairs={{0,8},{8,16},{16,24},{1,9},{9,17},{17,25},{2,10},{10,18},{18,26},{... | collective-permute-start | bytes 786440 | tf_op jit(solution)/shard_map/ppermute | solution.py:18
  40.3 1.3 collective-permute-start.5
  41.6 2.6 collective-permute-done.4
  44.1 4.4 %collective-permute-done.5 = bf16[1,4,128,256]{3,2,1,0:T(8,128)(2,1)S(1)} collective-permute-done((bf16[1,4,128,256]{3,2,1,0:T(8,128)(2,1)S(1)}, bf16[1,4,128,256]{3,2,1,0:T(8,128)(2,1)S(1)}, u32[]{:S(2)}, u32[]{:S(2)}) %collective-permute-start.5) | collective-permute-done | bytes 262176 | tf_op jit(solution)/shard_map/ppermute | solution.py:20
  48.5 0.8 pad_maximum_fusion.29
  49.3 5.3 %collective-permute-start.6 = (bf16[3,1,128,256]{3,2,1,0:T(8,128)(2,1)}, bf16[3,1,128,256]{3,2,1,0:T(8,128)(2,1)}, u32[]{:S(2)}, u32[]{:S(2)}) collective-permute-start(bf16[3,1,128,256]{3,2,1,0:T(8,128)(2,1)} %get-tuple-element.246), channel_id=1, source_target_pairs={{0,1},{1,2},{2,3},{3,4},{4,5},{5,6},{6,7},{8,9},{9,10},{10,11},{11... | collective-permute-start | bytes 589832 | tf_op jit(solution)/shard_map/ppermute | solution.py:18
  54.6 1.5 collective-permute-start.7
  56.1 1.7 fusion.101
  58.4 1.2 collective-permute-done.7
  59.6 1.5 select_maximum_fusion.1
  61.1 0.8 fusion.104
  62.0 1.1 fusion.35
  63.6 0.5 copy-done.8
  64.8 0.7 copy-done.7
  66.3 0.6 copy-done.11
  67.8 0.6 copy-done.4
  68.8 0.5 copy-done.3
  69.7 0.4 broadcast_multiply_fusion
  70.8 2.2 fusion.98
  73.5 1.2 fusion.31
  74.7 15.0 %all_gather.9 = bf16[1024,128]{1,0:T(8,128)(2,1)S(1)} all-gather(bf16[128,128]{1,0:T(8,128)(2,1)S(1)} %fusion.31), channel_id=1, replica_groups=mesh['aa'=4,'ba'=8] {'ba'}, dimensions={0}, use_global_device_ids=true | all-gather | bytes 294912 | tf_op jit(solution)/shard_map/all_gather | solution.py:134
  89.7 1.3 add_reduce_fusion
  91.0 1.2 multiply_reduce_fusion
  92.9 4.3 %fusion.25 = bf16[1024,768]{0,1:T(8,128)(2,1)S(1)} fusion(bf16[2048,256]{1,0:T(8,128)(2,1)S(1)} %copy-done.16, bf16[2048,256]{1,0:T(8,128)(2,1)S(1)} %copy-done.17, bf16[2048,256]{1,0:T(8,128)(2,1)S(1)} %copy-done.18, f32[1024,2048]{1,0:T(8,128)S(1)} %get-tuple-element.255, f32[2048]{0:T(1024)S(1)} %copy-done.19, f32[1024]{0:T(1024)S(1)} %add_rsqrt_fusion, ...), kind=kOutput, calls=%fused_computation.33 | convolution fusion | flops 3241934848 | bytes 13131776 | tf_op jit(solution)/shard_map/dot_general | solution.py:132
  97.2 1.1 fusion.103
  98.3 0.7 all-gather.5.cloned.1.call-update
  99.4 43.0 %all-gather.3.cloned.1.call-done = bf16[4096,256]{0,1:T(8,128)(2,1)} async-done(((bf16[1024,256]{0,1:T(8,128)(2,1)}), bf16[4096,256]{0,1:T(8,128)(2,1)}) %all-gather.3.cloned.1.call-update) | async-done | bytes 2097168 | tf_op jit(solution)/shard_map/all_gather | solution.py:75
  142.4 46.1 %all-gather.5.cloned.1.call-done = bf16[4096,256]{0,1:T(8,128)(2,1)} async-done(((bf16[1024,256]{0,1:T(8,128)(2,1)}), bf16[4096,256]{0,1:T(8,128)(2,1)}) %all-gather.5.cloned.1.call-update) | async-done | bytes 2097168 | tf_op jit(solution)/shard_map/all_gather | solution.py:76
  188.4 101.7 %while.18 = (s32[]{:T(128)}, f32[4,1024]{1,0:T(4,128)S(1)}, f32[4,1024]{1,0:T(4,128)S(1)}, f32[1024,4,64]{0,2,1:T(8,128)S(1)}, bf16[4096,256]{0,1:T(8,128)(2,1)}...) while((s32[]{:T(128)}, f32[4,1024]{1,0:T(4,128)S(1)}, ...), condition=%wide.region_5.6_spmd.clone, body=%wide.region_2.5_spmd.clone.sunk | while | flops 1108107264 | bytes 56361128 | solution.py:104
  188.4 1.3 constant_dynamic-slice_fusion.3
  189.7 8.1 %bitcast_reduce_fusion.2 = (f32[4,1024]{1,0:T(4,128)S(1)}, f32[4,1024,1024]{2,1,0:T(8,128)}) fusion(bf16[1024,4,64]{0,2,1:T(8,128)(2,1)S(1)} %bitcast.131, bf16[1024,4,64]{0,2,1:T(8,128)(2,1)S(1)} %get-tuple-element.340), kind=kOutput, calls=%fused_computation.1.clone.1 | convolution fusion | flops 545255424 | bytes 17842176 | tf_op jit(solution)/shard_map/while/body/eval_jaxpr/qhd,khd->hqk/dot_general | solution.py:89
  197.9 7.4 %fusion.168 = f32[1024,4,64]{0,2,1:T(8,128)S(1)} fusion(bf16[1024,4,64]{0,2,1:T(8,128)(2,1)S(1)} %bitcast.132, f32[4,1024,1024]{2,1,0:T(8,128)} %get-tuple-element.310, f32[4,1024]{1,0:T(4,128)S(1)} %get-tuple-element.336, f32[1024,4,64]{0,2,1:T(8,128)S(1)} %get-tuple-element.327, f32[1024,4]{0,1:T(4,128)S(1)} %get-tuple-element.312, pred[]{:T(512)S(6)} %compare.43), kind=kOutput, calls=%fused_computation.7.clone.1 | convolution fusion | flops 550240256 | bytes 19431424 | tf_op jit(solution)/shard_map/while/body/eval_jaxpr/hqk,khd->qhd/dot_general | solution.py:96
  205.2 8.5 %fusion.166 = f32[4,1024]{1,0:T(4,128)S(1)} fusion(f32[4,1024,1024]{2,1,0:T(8,128)} %get-tuple-element.310, f32[4,1024]{1,0:T(4,128)S(1)} %get-tuple-element.336), kind=kLoop, calls=%fused_computation.4.clone.1 | loop fusion | flops 12578816 | bytes 16809984 | tf_op jit(solution)/shard_map/while/body/eval_jaxpr/reduce_sum | solution.py:95
  213.8 1.3 constant_dynamic-slice_fusion.3
  215.1 8.1 %bitcast_reduce_fusion.2 = (f32[4,1024]{1,0:T(4,128)S(1)}, f32[4,1024,1024]{2,1,0:T(8,128)}) fusion(bf16[1024,4,64]{0,2,1:T(8,128)(2,1)S(1)} %bitcast.131, bf16[1024,4,64]{0,2,1:T(8,128)(2,1)S(1)} %get-tuple-element.340), kind=kOutput, calls=%fused_computation.1.clone.1 | convolution fusion | flops 545255424 | bytes 17842176 | tf_op jit(solution)/shard_map/while/body/eval_jaxpr/qhd,khd->hqk/dot_general | solution.py:89
  223.3 7.4 %fusion.168 = f32[1024,4,64]{0,2,1:T(8,128)S(1)} fusion(bf16[1024,4,64]{0,2,1:T(8,128)(2,1)S(1)} %bitcast.132, f32[4,1024,1024]{2,1,0:T(8,128)} %get-tuple-element.310, f32[4,1024]{1,0:T(4,128)S(1)} %get-tuple-element.336, f32[1024,4,64]{0,2,1:T(8,128)S(1)} %get-tuple-element.327, f32[1024,4]{0,1:T(4,128)S(1)} %get-tuple-element.312, pred[]{:T(512)S(6)} %compare.43), kind=kOutput, calls=%fused_computation.7.clone.1 | convolution fusion | flops 550240256 | bytes 19431424 | tf_op jit(solution)/shard_map/while/body/eval_jaxpr/hqk,khd->qhd/dot_general | solution.py:96
  230.7 8.5 %fusion.166 = f32[4,1024]{1,0:T(4,128)S(1)} fusion(f32[4,1024,1024]{2,1,0:T(8,128)} %get-tuple-element.310, f32[4,1024]{1,0:T(4,128)S(1)} %get-tuple-element.336), kind=kLoop, calls=%fused_computation.4.clone.1 | loop fusion | flops 12578816 | bytes 16809984 | tf_op jit(solution)/shard_map/while/body/eval_jaxpr/reduce_sum | solution.py:95
  239.3 1.3 constant_dynamic-slice_fusion.3
  240.5 8.1 %bitcast_reduce_fusion.2 = (f32[4,1024]{1,0:T(4,128)S(1)}, f32[4,1024,1024]{2,1,0:T(8,128)}) fusion(bf16[1024,4,64]{0,2,1:T(8,128)(2,1)S(1)} %bitcast.131, bf16[1024,4,64]{0,2,1:T(8,128)(2,1)S(1)} %get-tuple-element.340), kind=kOutput, calls=%fused_computation.1.clone.1 | convolution fusion | flops 545255424 | bytes 17842176 | tf_op jit(solution)/shard_map/while/body/eval_jaxpr/qhd,khd->hqk/dot_general | solution.py:89
  248.7 7.4 %fusion.168 = f32[1024,4,64]{0,2,1:T(8,128)S(1)} fusion(bf16[1024,4,64]{0,2,1:T(8,128)(2,1)S(1)} %bitcast.132, f32[4,1024,1024]{2,1,0:T(8,128)} %get-tuple-element.310, f32[4,1024]{1,0:T(4,128)S(1)} %get-tuple-element.336, f32[1024,4,64]{0,2,1:T(8,128)S(1)} %get-tuple-element.327, f32[1024,4]{0,1:T(4,128)S(1)} %get-tuple-element.312, pred[]{:T(512)S(6)} %compare.43), kind=kOutput, calls=%fused_computation.7.clone.1 | convolution fusion | flops 550240256 | bytes 19431424 | tf_op jit(solution)/shard_map/while/body/eval_jaxpr/hqk,khd->qhd/dot_general | solution.py:96
  256.1 8.5 %fusion.166 = f32[4,1024]{1,0:T(4,128)S(1)} fusion(f32[4,1024,1024]{2,1,0:T(8,128)} %get-tuple-element.310, f32[4,1024]{1,0:T(4,128)S(1)} %get-tuple-element.336), kind=kLoop, calls=%fused_computation.4.clone.1 | loop fusion | flops 12578816 | bytes 16809984 | tf_op jit(solution)/shard_map/while/body/eval_jaxpr/reduce_sum | solution.py:95
  264.7 1.3 constant_dynamic-slice_fusion.3
  266.0 8.1 %bitcast_reduce_fusion.2 = (f32[4,1024]{1,0:T(4,128)S(1)}, f32[4,1024,1024]{2,1,0:T(8,128)}) fusion(bf16[1024,4,64]{0,2,1:T(8,128)(2,1)S(1)} %bitcast.131, bf16[1024,4,64]{0,2,1:T(8,128)(2,1)S(1)} %get-tuple-element.340), kind=kOutput, calls=%fused_computation.1.clone.1 | convolution fusion | flops 545255424 | bytes 17842176 | tf_op jit(solution)/shard_map/while/body/eval_jaxpr/qhd,khd->hqk/dot_general | solution.py:89
  274.1 7.4 %fusion.168 = f32[1024,4,64]{0,2,1:T(8,128)S(1)} fusion(bf16[1024,4,64]{0,2,1:T(8,128)(2,1)S(1)} %bitcast.132, f32[4,1024,1024]{2,1,0:T(8,128)} %get-tuple-element.310, f32[4,1024]{1,0:T(4,128)S(1)} %get-tuple-element.336, f32[1024,4,64]{0,2,1:T(8,128)S(1)} %get-tuple-element.327, f32[1024,4]{0,1:T(4,128)S(1)} %get-tuple-element.312, pred[]{:T(512)S(6)} %compare.43), kind=kOutput, calls=%fused_computation.7.clone.1 | convolution fusion | flops 550240256 | bytes 19431424 | tf_op jit(solution)/shard_map/while/body/eval_jaxpr/hqk,khd->qhd/dot_general | solution.py:96
  281.5 8.5 %fusion.166 = f32[4,1024]{1,0:T(4,128)S(1)} fusion(f32[4,1024,1024]{2,1,0:T(8,128)} %get-tuple-element.310, f32[4,1024]{1,0:T(4,128)S(1)} %get-tuple-element.336), kind=kLoop, calls=%fused_computation.4.clone.1 | loop fusion | flops 12578816 | bytes 16809984 | tf_op jit(solution)/shard_map/while/body/eval_jaxpr/reduce_sum | solution.py:95
  290.2 0.7 copy-done.13
  290.9 1.0 convolution_convert_fusion
  292.0 32.6 %reduce-scatter.2.cloned.1.call-done = bf16[128,128]{1,0:T(8,128)(2,1)} async-done(((bf16[1024,128]{1,0:T(8,128)(2,1)}), bf16[128,128]{1,0:T(8,128)(2,1)}) %reduce-scatter.2.cloned.1.call-update) | async-done | bytes 32784 | tf_op jit(solution)/shard_map/reduce_scatter | solution.py:140
  324.6 1.4 convert_element_type.90
  (92 shorter events, 9.8 us)
Async XLA Ops:
  6.5 83.1 %copy-start = (bf16[128,2048]{1,0:T(8,128)(2,1)S(1)}, bf16[128,2048]{1,0:T(8,128)(2,1)}, u32[]{:S(2)}) copy-start(bf16[128,2048]{1,0:T(8,128)(2,1)} %param.23) | copy-start | bytes 1572868
  6.5 135.8 %all-gather.3.cloned.1.call-start = ((), (), s32[]{:S(2)}) async-start(), calls=%async_computation.1 | async-start | bytes 2621440 | tf_op jit(solution)/shard_map/all_gather | solution.py:75
  6.5 10.9 %collective-permute-start = (bf16[1,4,128,256]{3,2,1,0:T(8,128)(2,1)}, bf16[1,4,128,256]{3,2,1,0:T(8,128)(2,1)S(1)}, u32[]{:S(2)}, u32[]{:S(2)}) collective-permute-start(bf16[1,4,128,256]{3,2,1,0:T(8,128)(2,1)} %param.16), channel_id=1, source_target_pairs={{0,8},{8,16},{16,24},{1,9},{9,17},{17,25},{2,10},{10,18},{18,26},{... | collective-permute-start | bytes 786440 | tf_op jit(solution)/shard_map/ppermute | solution.py:18
  11.6 9.9 %collective-permute-start.1 = (bf16[1,4,128,256]{3,2,1,0:T(8,128)(2,1)}, bf16[1,4,128,256]{3,2,1,0:T(8,128)(2,1)S(1)}, u32[]{:S(2)}, u32[]{:S(2)}) collective-permute-start(bf16[1,4,128,256]{3,2,1,0:T(8,128)(2,1)} %param.16), channel_id=1, source_target_pairs={{8,0},{16,8},{24,16},{9,1},{17,9},{25,17},{10,2},{18,10},{26,18},{... | collective-permute-start | bytes 786440 | tf_op jit(solution)/shard_map/ppermute | solution.py:20
  21.6 4.8 %collective-permute-start.2 = (bf16[3,1,128,256]{3,2,1,0:T(8,128)(2,1)S(1)}, bf16[3,1,128,256]{3,2,1,0:T(8,128)(2,1)S(1)}, u32[]{:S(2)}, u32[]{:S(2)}) collective-permute-start(bf16[3,1,128,256]{3,2,1,0:T(8,128)(2,1)S(1)} %get-tuple-element.248), channel_id=1, source_target_pairs={{0,1},{1,2},{2,3},{3,4},{4,5},{5,6},{6,7},{8,9},{9,10},{10,11},{11... | collective-permute-start | bytes 589832 | tf_op jit(solution)/shard_map/ppermute | solution.py:18
  22.9 5.1 %collective-permute-start.3 = (bf16[3,1,128,256]{3,2,1,0:T(8,128)(2,1)S(1)}, bf16[3,1,128,256]{3,2,1,0:T(8,128)(2,1)S(1)}, u32[]{:S(2)}, u32[]{:S(2)}) collective-permute-start(bf16[3,1,128,256]{3,2,1,0:T(8,128)(2,1)S(1)} %get-tuple-element.247), channel_id=1, source_target_pairs={{1,0},{2,1},{3,2},{4,3},{5,4},{6,5},{7,6},{9,8},{10,9},{11,10},{12... | collective-permute-start | bytes 589832 | tf_op jit(solution)/shard_map/ppermute | solution.py:20
  28.5 1.0 copy-start.10
  32.9 0.7 copy-start.20
  33.6 22.5 %copy-start.2 = (bf16[3,3,3,256,256]{4,3,2,1,0:T(8,128)(2,1)S(1)}, bf16[3,3,3,256,256]{4,3,2,1,0:T(8,128)(2,1)}, u32[]{:S(2)}) copy-start(bf16[3,3,3,256,256]{4,3,2,1,0:T(8,128)(2,1)} %param.19) | copy-start | bytes 10616836
  36.8 7.3 %collective-permute-start.4 = (bf16[1,4,128,256]{3,2,1,0:T(8,128)(2,1)S(1)}, bf16[1,4,128,256]{3,2,1,0:T(8,128)(2,1)S(1)}, u32[]{:S(2)}, u32[]{:S(2)}) collective-permute-start(bf16[1,4,128,256]{3,2,1,0:T(8,128)(2,1)S(1)} %fusion.66), channel_id=1, source_target_pairs={{0,8},{8,16},{16,24},{1,9},{9,17},{17,25},{2,10},{10,18},{18,26},{... | collective-permute-start | bytes 786440 | tf_op jit(solution)/shard_map/ppermute | solution.py:18
  40.3 8.3 %collective-permute-start.5 = (bf16[1,4,128,256]{3,2,1,0:T(8,128)(2,1)S(1)}, bf16[1,4,128,256]{3,2,1,0:T(8,128)(2,1)S(1)}, u32[]{:S(2)}, u32[]{:S(2)}) collective-permute-start(bf16[1,4,128,256]{3,2,1,0:T(8,128)(2,1)S(1)} %fusion.66), channel_id=1, source_target_pairs={{8,0},{16,8},{24,16},{9,1},{17,9},{25,17},{10,2},{18,10},{26,18},{... | collective-permute-start | bytes 786440 | tf_op jit(solution)/shard_map/ppermute | solution.py:20
  49.3 9.1 %collective-permute-start.6 = (bf16[3,1,128,256]{3,2,1,0:T(8,128)(2,1)}, bf16[3,1,128,256]{3,2,1,0:T(8,128)(2,1)}, u32[]{:S(2)}, u32[]{:S(2)}) collective-permute-start(bf16[3,1,128,256]{3,2,1,0:T(8,128)(2,1)} %get-tuple-element.246), channel_id=1, source_target_pairs={{0,1},{1,2},{2,3},{3,4},{4,5},{5,6},{6,7},{8,9},{9,10},{10,11},{11... | collective-permute-start | bytes 589832 | tf_op jit(solution)/shard_map/ppermute | solution.py:18
  54.6 5.0 %collective-permute-start.7 = (bf16[3,1,128,256]{3,2,1,0:T(8,128)(2,1)}, bf16[3,1,128,256]{3,2,1,0:T(8,128)(2,1)S(1)}, u32[]{:S(2)}, u32[]{:S(2)}) collective-permute-start(bf16[3,1,128,256]{3,2,1,0:T(8,128)(2,1)} %get-tuple-element.245), channel_id=1, source_target_pairs={{1,0},{2,1},{3,2},{4,3},{5,4},{6,5},{7,6},{9,8},{10,9},{11,10},{12... | collective-permute-start | bytes 589832 | tf_op jit(solution)/shard_map/ppermute | solution.py:20
  62.0 1.1 copy-start.9
  63.1 1.0 copy-start.8
  64.5 1.0 copy-start.7
  64.8 1.1 copy-start.6
  65.9 1.0 copy-start.11
  65.9 1.1 copy-start.21
  66.3 1.1 copy-start.5
  67.3 1.0 copy-start.4
  68.3 1.0 copy-start.3
  68.7 1.0 copy-start.14
  70.8 2.7 copy-start.15
  70.8 18.9 %copy-start.12 = (f32[2048]{0:T(1024)S(1)}, f32[2048]{0:T(1024)}, u32[]{:S(2)}) copy-start(f32[2048]{0:T(1024)} %param.24) | copy-start | bytes 24580
  91.0 1.3 copy-start.16
  91.0 1.5 copy-start.17
  91.0 1.8 copy-start.18
  91.0 1.8 copy-start.19
  98.3 90.1 %all-gather.5.cloned.1.call-start = ((), (), s32[]{:S(2)}) async-start(), calls=%async_computation.2 | async-start | bytes 2621440 | tf_op jit(solution)/shard_map/all_gather | solution.py:76
  99.1 225.6 %reduce-scatter.2.cloned.1.call-start = ((), (), s32[]{:S(2)}) async-start(), calls=%async_computation.3 | async-start | bytes 294912 | tf_op jit(solution)/shard_map/reduce_scatter | solution.py:140
  290.1 0.8 copy-start.13
  290.1 35.9 %copy-start.1 = (bf16[128,2048]{1,0:T(8,128)(2,1)S(1)}, bf16[128,2048]{1,0:T(8,128)(2,1)}, u32[]{:S(2)}) copy-start(bf16[128,2048]{1,0:T(8,128)(2,1)} %param.23) | copy-start | bytes 1572868
Sparse Core Ops, SparseCore 0:
  98.4 43.8 all-gather.2
  143.9 44.4 all-gather.4
  292.1 32.4 reduce-scatter.1
where the time goes:
time: 334 us; the launch traced here: 333 us
  waiting for transfers between devices  140 us (42%)
  matrix products  78.4 us (23%)
  other arithmetic  45.5 us (14%)
  starting transfers between devices  20.9 us (6%)
  local copies, waits for them, and re-layouts  19.1 us (6%)
  blocking collectives  15 us (4%)
  between operations  13.7 us (4%)
    all_gather x1, waiting for transfers between devices, attend(): value_rows = lax.all_gather(values, 'aa', axis=0, tiled=True)  46.1 us
    all_gather x1, waiting for transfers between devices, attend(): key_rows = lax.all_gather(keys, 'aa', axis=0, tiled=True)  43 us
    reduce_sum x4, other arithmetic, one_step(): denom = denom * fade + probs.sum(-1)  34.1 us
    reduce_scatter x1, waiting for transfers between devices, on_device(): lax.psum_scatter(jnp.dot(attended, w_velocity, preferred_element_type=jnp...  32.6 us
    dot_general x4, matrix products, one_step(): jnp.einsum('qhd,khd->hqk', query_heads, key_block, preferred_element_type...  32.6 us
    dot_general x4, matrix products, one_step(): jnp.einsum('hqk,khd->qhd', probs.astype(jnp.bfloat16), value_block, prefe...  29.5 us
    ppermute x4, starting transfers between devices, with_halo(): lax.ppermute(tail, axis, [(i, (i + 1) % count) for i in range(ends)])  15.2 us
    all_gather x1, blocking collectives, on_device(): lax.all_gather(latents, 'ba', axis=0, tiled=True)  15 us
  transfers between devices with their start and end apart: 11, of which 9 were waited for; matrix products, arithmetic and copies ran while one was open for 2% of the time, Pallas kernels for 0%

commit v1 on v0

--- a/solution.py
+++ b/solution.py
@@ -72,7 +72,14 @@
         jnp.zeros((heads, rows), jnp.float32),
         jnp.zeros((rows, heads, HEAD_DIM), jnp.float32),
     )
-    key_rows = lax.all_gather(keys, "aa", axis=0, tiled=True)
+    ways, here, hop = (lax.axis_size("aa"), lax.axis_index("aa"), keys.shape[0])
+    line, have = (keys, 1)
+    while have < ways:
+        line = jnp.concatenate(
+            [line, lax.ppermute(line, "aa", [(d, (d - have) % ways) for d in range(ways)])], axis=0
+        )
+        have = 2 * have
+    key_rows = jnp.roll(line, here * hop, axis=0)
     value_rows = lax.all_gather(values, "aa", axis=0, tiled=True)
     count = key_rows.shape[0]
     block = math.gcd(count, 1024)

time: 334 us -> 352 us (1.054)
  waiting for transfers between devices: 140 us -> 150 us
  local copies, waits for them, and re-layouts: 19.1 us -> 26.2 us
    ppermute x0 -> x2, waiting for transfers between devices: none -> 60.5 us  [attend(): lax.ppermute(line, 'aa', [(d, (d - have) % ways) for d in range(ways)])]
    all_gather x1 -> x0, waiting for transfers between devices: 43 us -> none  [attend(): key_rows = lax.all_gather(keys, 'aa', axis=0, tiled=True)]
    all_gather x1, waiting for transfers between devices: 46.1 us -> 39.1 us  [attend(): value_rows = lax.all_gather(values, 'aa', axis=0, tiled=True)]
    unnamed x46 -> x57, local copies, waits for them, and re-layouts: 5.63 us -> 8.55 us
  transfers between devices with their start and end apart: 11 -> 12, of which waited for: 9 -> 10; matrix products, arithmetic and copies ran while one was open for 2% -> 3% of each run, Pallas kernels for 0% -> 0%
where the time goes in v1:
time: 352 us; the launch traced here: 351 us
  waiting for transfers between devices  150 us (43%)
  matrix products  77.5 us (22%)
  other arithmetic  45.6 us (13%)
  local copies, waits for them, and re-layouts  26.2 us (7%)
  starting transfers between devices  22.5 us (6%)
  blocking collectives  15 us (4%)
  between operations  14.1 us (4%)
    ppermute x2, waiting for transfers between devices, attend(): lax.ppermute(line, 'aa', [(d, (d - have) % ways) for d in range(ways)])  60.5 us
    all_gather x1, waiting for transfers between devices, attend(): value_rows = lax.all_gather(values, 'aa', axis=0, tiled=True)  39.1 us
    reduce_sum x4, other arithmetic, one_step(): denom = denom * fade + probs.sum(-1)  34.1 us
    reduce_scatter x1, waiting for transfers between devices, on_device(): lax.psum_scatter(jnp.dot(attended, w_velocity, preferred_element_type=jnp...  32.6 us
    dot_general x4, matrix products, one_step(): jnp.einsum('qhd,khd->hqk', query_heads, key_block, preferred_element_type...  32.6 us
    dot_general x4, matrix products, one_step(): jnp.einsum('hqk,khd->qhd', probs.astype(jnp.bfloat16), value_block, prefe...  29.5 us
    ppermute x4, starting transfers between devices, with_halo(): lax.ppermute(tail, axis, [(i, (i + 1) % count) for i in range(ends)])  15.2 us
    all_gather x1, blocking collectives, on_device(): lax.all_gather(latents, 'ba', axis=0, tiled=True)  15 us
  transfers between devices with their start and end apart: 12, of which 10 were waited for; matrix products, arithmetic and copies ran while one was open for 3% of the time, Pallas kernels for 0%

profile of v1, /device:TPU:0, one launch (start us, length us, event | category | flops | bytes accessed | tf_op | source)
XLA Modules:
  0.0 350.8 jit_solution(7876135027988444750)
XLA Ops:
  6.5 5.1 %collective-permute-start = (bf16[1,4,128,256]{3,2,1,0:T(8,128)(2,1)}, bf16[1,4,128,256]{3,2,1,0:T(8,128)(2,1)S(1)}, u32[]{:S(2)}, u32[]{:S(2)}) collective-permute-start(bf16[1,4,128,256]{3,2,1,0:T(8,128)(2,1)} %param.16), channel_id=1, source_target_pairs={{0,8},{8,16},{16,24},{1,9},{9,17},{17,25},{2,10},{10,18},{18,26},{... | collective-permute-start | bytes 786440 | tf_op jit(solution)/shard_map/ppermute | solution.py:18
  11.6 1.3 collective-permute-start.1
  12.9 4.5 %collective-permute-done = bf16[1,4,128,256]{3,2,1,0:T(8,128)(2,1)S(1)} collective-permute-done((bf16[1,4,128,256]{3,2,1,0:T(8,128)(2,1)}, bf16[1,4,128,256]{3,2,1,0:T(8,128)(2,1)S(1)}, u32[]{:S(2)}, u32[]{:S(2)}) %collective-permute-start) | collective-permute-done | bytes 262176 | tf_op jit(solution)/shard_map/ppermute | solution.py:18
  17.5 1.0 constant_dynamic-update-slice_fusion.1
  18.5 3.0 collective-permute-done.1
  21.6 1.3 collective-permute-start.2
  22.9 1.3 collective-permute-start.3
  24.2 2.2 fusion.102
  26.4 1.6 collective-permute-done.3
  27.9 0.6 select_maximum_fusion.5
  28.5 0.9 fusion.106
  33.5 2.1 fusion.69
  35.7 1.1 fusion.66
  36.8 3.5 collective-permute-start.4
  40.3 1.3 collective-permute-start.5
  41.6 2.6 collective-permute-done.4
  44.1 4.4 %collective-permute-done.5 = bf16[1,4,128,256]{3,2,1,0:T(8,128)(2,1)S(1)} collective-permute-done((bf16[1,4,128,256]{3,2,1,0:T(8,128)(2,1)S(1)}, bf16[1,4,128,256]{3,2,1,0:T(8,128)(2,1)S(1)}, u32[]{:S(2)}, u32[]{:S(2)}) %collective-permute-start.5) | collective-permute-done | bytes 262176 | tf_op jit(solution)/shard_map/ppermute | solution.py:20
  48.5 0.8 pad_maximum_fusion.30
  49.3 5.3 %collective-permute-start.6 = (bf16[3,1,128,256]{3,2,1,0:T(8,128)(2,1)}, bf16[3,1,128,256]{3,2,1,0:T(8,128)(2,1)}, u32[]{:S(2)}, u32[]{:S(2)}) collective-permute-start(bf16[3,1,128,256]{3,2,1,0:T(8,128)(2,1)} %get-tuple-element.248), channel_id=1, source_target_pairs={{0,1},{1,2},{2,3},{3,4},{4,5},{5,6},{6,7},{8,9},{9,10},{10,11},{11... | collective-permute-start | bytes 589832 | tf_op jit(solution)/shard_map/ppermute | solution.py:18
  54.6 1.5 collective-permute-start.7
  56.1 1.6 fusion.101
  58.4 1.3 collective-permute-done.7
  59.7 1.6 select_maximum_fusion.1
  61.2 0.9 fusion.105
  62.1 1.1 fusion.35
  65.0 0.7 copy-done.8
  66.4 0.6 copy-done.14
  67.9 0.6 copy-done.5
  68.9 0.5 copy-done.4
  70.9 2.2 fusion.98
  73.8 15.0 %all_gather.6 = bf16[1024,128]{1,0:T(8,128)(2,1)S(1)} all-gather(bf16[128,128]{1,0:T(8,128)(2,1)S(1)} %fusion.31), channel_id=1, replica_groups=mesh['aa'=4,'ba'=8] {'ba'}, dimensions={0}, use_global_device_ids=true | all-gather | bytes 294912 | tf_op jit(solution)/shard_map/all_gather | solution.py:141
  88.9 1.3 add_reduce_fusion
  90.2 1.2 multiply_reduce_fusion
  92.1 4.3 %fusion.25 = bf16[1024,768]{0,1:T(8,128)(2,1)S(1)} fusion(bf16[2048,256]{1,0:T(8,128)(2,1)S(1)} %copy-done.20, bf16[2048,256]{1,0:T(8,128)(2,1)S(1)} %copy-done.21, bf16[2048,256]{1,0:T(8,128)(2,1)S(1)} %copy-done.22, f32[1024,2048]{1,0:T(8,128)S(1)} %get-tuple-element.257, f32[2048]{0:T(1024)S(1)} %copy-done.23, f32[1024]{0:T(1024)S(1)} %add_rsqrt_fusion, ...), kind=kOutput, calls=%fused_computation.33 | convolution fusion | flops 3241934848 | bytes 13131776 | tf_op jit(solution)/shard_map/dot_general | solution.py:139
  96.8 13.9 %collective-permute-done.8 = bf16[1024,256]{0,1:T(8,128)(2,1)S(1)} collective-permute-done((bf16[1024,256]{0,1:T(8,128)(2,1)S(1)}, bf16[1024,256]{0,1:T(8,128)(2,1)S(1)}, u32[]{:S(2)}, u32[]{:S(2)}) %collective-permute-start.8) | collective-permute-done | bytes 524320 | tf_op jit(solution)/shard_map/ppermute | solution.py:79
  110.8 1.4 collective-permute-start.9
  112.1 46.6 %collective-permute-done.9 = bf16[2048,256]{0,1:T(8,128)(2,1)S(1)} collective-permute-done((bf16[2048,256]{0,1:T(8,128)(2,1)S(1)}, bf16[2048,256]{0,1:T(8,128)(2,1)S(1)}, u32[]{:S(2)}, u32[]{:S(2)}) %collective-permute-start.9) | collective-permute-done | bytes 1048608 | tf_op jit(solution)/shard_map/ppermute | solution.py:79
  158.8 0.9 fusion.103
  159.8 2.0 copy-done.3
  162.1 0.9 constant_dynamic-update-slice_fusion.4
  163.0 1.1 constant_dynamic-update-slice_fusion.3
  164.1 3.1 constant_dynamic-slice_fusion.2
  167.2 39.1 %all-gather.2.cloned.1.call-done = bf16[4096,256]{0,1:T(8,128)(2,1)} async-done(((bf16[1024,256]{0,1:T(8,128)(2,1)}), bf16[4096,256]{0,1:T(8,128)(2,1)}) %all-gather.2.cloned.1.call-update) | async-done | bytes 2097168 | tf_op jit(solution)/shard_map/all_gather | solution.py:83
  206.3 101.7 %while.18 = (s32[]{:T(128)}, f32[4,1024]{1,0:T(4,128)S(1)}, f32[4,1024]{1,0:T(4,128)S(1)}, f32[1024,4,64]{0,2,1:T(8,128)S(1)}, bf16[4096,256]{0,1:T(8,128)(2,1)}...) while((s32[]{:T(128)}, f32[4,1024]{1,0:T(4,128)S(1)}, ...), condition=%wide.region_5.6_spmd.clone, body=%wide.region_2.5_spmd.clone.sunk | while | flops 1108107264 | bytes 56361128 | solution.py:111
  206.3 1.3 constant_dynamic-slice_fusion.4
  207.6 8.1 %bitcast_reduce_fusion.2 = (f32[4,1024]{1,0:T(4,128)S(1)}, f32[4,1024,1024]{2,1,0:T(8,128)}) fusion(bf16[1024,4,64]{0,2,1:T(8,128)(2,1)S(1)} %bitcast.131, bf16[1024,4,64]{0,2,1:T(8,128)(2,1)S(1)} %get-tuple-element.342), kind=kOutput, calls=%fused_computation.1.clone.1 | convolution fusion | flops 545255424 | bytes 17842176 | tf_op jit(solution)/shard_map/while/body/eval_jaxpr/qhd,khd->hqk/dot_general | solution.py:96
  215.7 7.4 %fusion.169 = f32[1024,4,64]{0,2,1:T(8,128)S(1)} fusion(bf16[1024,4,64]{0,2,1:T(8,128)(2,1)S(1)} %bitcast.132, f32[4,1024,1024]{2,1,0:T(8,128)} %get-tuple-element.312, f32[4,1024]{1,0:T(4,128)S(1)} %get-tuple-element.338, f32[1024,4,64]{0,2,1:T(8,128)S(1)} %get-tuple-element.329, f32[1024,4]{0,1:T(4,128)S(1)} %get-tuple-element.314, pred[]{:T(512)S(6)} %compare.44), kind=kOutput, calls=%fused_computation.7.clone.1 | convolution fusion | flops 550240256 | bytes 19431424 | tf_op jit(solution)/shard_map/while/body/eval_jaxpr/hqk,khd->qhd/dot_general | solution.py:103
  223.1 8.5 %fusion.167 = f32[4,1024]{1,0:T(4,128)S(1)} fusion(f32[4,1024,1024]{2,1,0:T(8,128)} %get-tuple-element.312, f32[4,1024]{1,0:T(4,128)S(1)} %get-tuple-element.338), kind=kLoop, calls=%fused_computation.4.clone.1 | loop fusion | flops 12578816 | bytes 16809984 | tf_op jit(solution)/shard_map/while/body/eval_jaxpr/reduce_sum | solution.py:102
  231.7 1.3 constant_dynamic-slice_fusion.4
  233.0 8.1 %bitcast_reduce_fusion.2 = (f32[4,1024]{1,0:T(4,128)S(1)}, f32[4,1024,1024]{2,1,0:T(8,128)}) fusion(bf16[1024,4,64]{0,2,1:T(8,128)(2,1)S(1)} %bitcast.131, bf16[1024,4,64]{0,2,1:T(8,128)(2,1)S(1)} %get-tuple-element.342), kind=kOutput, calls=%fused_computation.1.clone.1 | convolution fusion | flops 545255424 | bytes 17842176 | tf_op jit(solution)/shard_map/while/body/eval_jaxpr/qhd,khd->hqk/dot_general | solution.py:96
  241.2 7.4 %fusion.169 = f32[1024,4,64]{0,2,1:T(8,128)S(1)} fusion(bf16[1024,4,64]{0,2,1:T(8,128)(2,1)S(1)} %bitcast.132, f32[4,1024,1024]{2,1,0:T(8,128)} %get-tuple-element.312, f32[4,1024]{1,0:T(4,128)S(1)} %get-tuple-element.338, f32[1024,4,64]{0,2,1:T(8,128)S(1)} %get-tuple-element.329, f32[1024,4]{0,1:T(4,128)S(1)} %get-tuple-element.314, pred[]{:T(512)S(6)} %compare.44), kind=kOutput, calls=%fused_computation.7.clone.1 | convolution fusion | flops 550240256 | bytes 19431424 | tf_op jit(solution)/shard_map/while/body/eval_jaxpr/hqk,khd->qhd/dot_general | solution.py:103
  248.6 8.5 %fusion.167 = f32[4,1024]{1,0:T(4,128)S(1)} fusion(f32[4,1024,1024]{2,1,0:T(8,128)} %get-tuple-element.312, f32[4,1024]{1,0:T(4,128)S(1)} %get-tuple-element.338), kind=kLoop, calls=%fused_computation.4.clone.1 | loop fusion | flops 12578816 | bytes 16809984 | tf_op jit(solution)/shard_map/while/body/eval_jaxpr/reduce_sum | solution.py:102
  257.1 1.3 constant_dynamic-slice_fusion.4
  258.4 8.1 %bitcast_reduce_fusion.2 = (f32[4,1024]{1,0:T(4,128)S(1)}, f32[4,1024,1024]{2,1,0:T(8,128)}) fusion(bf16[1024,4,64]{0,2,1:T(8,128)(2,1)S(1)} %bitcast.131, bf16[1024,4,64]{0,2,1:T(8,128)(2,1)S(1)} %get-tuple-element.342), kind=kOutput, calls=%fused_computation.1.clone.1 | convolution fusion | flops 545255424 | bytes 17842176 | tf_op jit(solution)/shard_map/while/body/eval_jaxpr/qhd,khd->hqk/dot_general | solution.py:96
  266.6 7.4 %fusion.169 = f32[1024,4,64]{0,2,1:T(8,128)S(1)} fusion(bf16[1024,4,64]{0,2,1:T(8,128)(2,1)S(1)} %bitcast.132, f32[4,1024,1024]{2,1,0:T(8,128)} %get-tuple-element.312, f32[4,1024]{1,0:T(4,128)S(1)} %get-tuple-element.338, f32[1024,4,64]{0,2,1:T(8,128)S(1)} %get-tuple-element.329, f32[1024,4]{0,1:T(4,128)S(1)} %get-tuple-element.314, pred[]{:T(512)S(6)} %compare.44), kind=kOutput, calls=%fused_computation.7.clone.1 | convolution fusion | flops 550240256 | bytes 19431424 | tf_op jit(solution)/shard_map/while/body/eval_jaxpr/hqk,khd->qhd/dot_general | solution.py:103
  274.0 8.5 %fusion.167 = f32[4,1024]{1,0:T(4,128)S(1)} fusion(f32[4,1024,1024]{2,1,0:T(8,128)} %get-tuple-element.312, f32[4,1024]{1,0:T(4,128)S(1)} %get-tuple-element.338), kind=kLoop, calls=%fused_computation.4.clone.1 | loop fusion | flops 12578816 | bytes 16809984 | tf_op jit(solution)/shard_map/while/body/eval_jaxpr/reduce_sum | solution.py:102
  282.6 1.3 constant_dynamic-slice_fusion.4
  283.8 8.1 %bitcast_reduce_fusion.2 = (f32[4,1024]{1,0:T(4,128)S(1)}, f32[4,1024,1024]{2,1,0:T(8,128)}) fusion(bf16[1024,4,64]{0,2,1:T(8,128)(2,1)S(1)} %bitcast.131, bf16[1024,4,64]{0,2,1:T(8,128)(2,1)S(1)} %get-tuple-element.342), kind=kOutput, calls=%fused_computation.1.clone.1 | convolution fusion | flops 545255424 | bytes 17842176 | tf_op jit(solution)/shard_map/while/body/eval_jaxpr/qhd,khd->hqk/dot_general | solution.py:96
  292.0 7.4 %fusion.169 = f32[1024,4,64]{0,2,1:T(8,128)S(1)} fusion(bf16[1024,4,64]{0,2,1:T(8,128)(2,1)S(1)} %bitcast.132, f32[4,1024,1024]{2,1,0:T(8,128)} %get-tuple-element.312, f32[4,1024]{1,0:T(4,128)S(1)} %get-tuple-element.338, f32[1024,4,64]{0,2,1:T(8,128)S(1)} %get-tuple-element.329, f32[1024,4]{0,1:T(4,128)S(1)} %get-tuple-element.314, pred[]{:T(512)S(6)} %compare.44), kind=kOutput, calls=%fused_computation.7.clone.1 | convolution fusion | flops 550240256 | bytes 19431424 | tf_op jit(solution)/shard_map/while/body/eval_jaxpr/hqk,khd->qhd/dot_general | solution.py:103
  299.4 8.5 %fusion.167 = f32[4,1024]{1,0:T(4,128)S(1)} fusion(f32[4,1024,1024]{2,1,0:T(8,128)} %get-tuple-element.312, f32[4,1024]{1,0:T(4,128)S(1)} %get-tuple-element.338), kind=kLoop, calls=%fused_computation.4.clone.1 | loop fusion | flops 12578816 | bytes 16809984 | tf_op jit(solution)/shard_map/while/body/eval_jaxpr/reduce_sum | solution.py:102
  308.1 0.7 copy-done.17
  308.8 1.1 convolution_convert_fusion
  309.9 32.6 %reduce-scatter.2.cloned.1.call-done = bf16[128,128]{1,0:T(8,128)(2,1)} async-done(((bf16[1024,128]{1,0:T(8,128)(2,1)}), bf16[128,128]{1,0:T(8,128)(2,1)}) %reduce-scatter.2.cloned.1.call-update) | async-done | bytes 32784 | tf_op jit(solution)/shard_map/reduce_scatter | solution.py:147
  342.5 1.4 convert_element_type.90
  (108 shorter events, 12.3 us)
Async XLA Ops:
  6.5 82.3 %copy-start = (bf16[128,2048]{1,0:T(8,128)(2,1)S(1)}, bf16[128,2048]{1,0:T(8,128)(2,1)}, u32[]{:S(2)}) copy-start(bf16[128,2048]{1,0:T(8,128)(2,1)} %param.23) | copy-start | bytes 1572868
  6.5 199.8 %all-gather.2.cloned.1.call-start = ((), (), s32[]{:S(2)}) async-start(), calls=%async_computation.1 | async-start | bytes 2621440 | tf_op jit(solution)/shard_map/all_gather | solution.py:83
  6.5 10.9 %collective-permute-start = (bf16[1,4,128,256]{3,2,1,0:T(8,128)(2,1)}, bf16[1,4,128,256]{3,2,1,0:T(8,128)(2,1)S(1)}, u32[]{:S(2)}, u32[]{:S(2)}) collective-permute-start(bf16[1,4,128,256]{3,2,1,0:T(8,128)(2,1)} %param.16), channel_id=1, source_target_pairs={{0,8},{8,16},{16,24},{1,9},{9,17},{17,25},{2,10},{10,18},{18,26},{... | collective-permute-start | bytes 786440 | tf_op jit(solution)/shard_map/ppermute | solution.py:18
  11.6 9.9 %collective-permute-start.1 = (bf16[1,4,128,256]{3,2,1,0:T(8,128)(2,1)}, bf16[1,4,128,256]{3,2,1,0:T(8,128)(2,1)S(1)}, u32[]{:S(2)}, u32[]{:S(2)}) collective-permute-start(bf16[1,4,128,256]{3,2,1,0:T(8,128)(2,1)} %param.16), channel_id=1, source_target_pairs={{8,0},{16,8},{24,16},{9,1},{17,9},{25,17},{10,2},{18,10},{26,18},{... | collective-permute-start | bytes 786440 | tf_op jit(solution)/shard_map/ppermute | solution.py:20
  21.6 4.8 %collective-permute-start.2 = (bf16[3,1,128,256]{3,2,1,0:T(8,128)(2,1)S(1)}, bf16[3,1,128,256]{3,2,1,0:T(8,128)(2,1)S(1)}, u32[]{:S(2)}, u32[]{:S(2)}) collective-permute-start(bf16[3,1,128,256]{3,2,1,0:T(8,128)(2,1)S(1)} %get-tuple-element.250), channel_id=1, source_target_pairs={{0,1},{1,2},{2,3},{3,4},{4,5},{5,6},{6,7},{8,9},{9,10},{10,11},{11... | collective-permute-start | bytes 589832 | tf_op jit(solution)/shard_map/ppermute | solution.py:18
  22.9 5.1 %collective-permute-start.3 = (bf16[3,1,128,256]{3,2,1,0:T(8,128)(2,1)S(1)}, bf16[3,1,128,256]{3,2,1,0:T(8,128)(2,1)S(1)}, u32[]{:S(2)}, u32[]{:S(2)}) collective-permute-start(bf16[3,1,128,256]{3,2,1,0:T(8,128)(2,1)S(1)} %get-tuple-element.249), channel_id=1, source_target_pairs={{1,0},{2,1},{3,2},{4,3},{5,4},{6,5},{7,6},{9,8},{10,9},{11,10},{12... | collective-permute-start | bytes 589832 | tf_op jit(solution)/shard_map/ppermute | solution.py:20
  28.5 1.0 copy-start.11
  32.9 0.7 copy-start.24
  33.5 22.6 %copy-start.2 = (bf16[3,3,3,256,256]{4,3,2,1,0:T(8,128)(2,1)S(1)}, bf16[3,3,3,256,256]{4,3,2,1,0:T(8,128)(2,1)}, u32[]{:S(2)}) copy-start(bf16[3,3,3,256,256]{4,3,2,1,0:T(8,128)(2,1)} %param.19) | copy-start | bytes 10616836
  36.8 7.3 %collective-permute-start.4 = (bf16[1,4,128,256]{3,2,1,0:T(8,128)(2,1)S(1)}, bf16[1,4,128,256]{3,2,1,0:T(8,128)(2,1)S(1)}, u32[]{:S(2)}, u32[]{:S(2)}) collective-permute-start(bf16[1,4,128,256]{3,2,1,0:T(8,128)(2,1)S(1)} %fusion.66), channel_id=1, source_target_pairs={{0,8},{8,16},{16,24},{1,9},{9,17},{17,25},{2,10},{10,18},{18,26},{... | collective-permute-start | bytes 786440 | tf_op jit(solution)/shard_map/ppermute | solution.py:18
  40.3 8.3 %collective-permute-start.5 = (bf16[1,4,128,256]{3,2,1,0:T(8,128)(2,1)S(1)}, bf16[1,4,128,256]{3,2,1,0:T(8,128)(2,1)S(1)}, u32[]{:S(2)}, u32[]{:S(2)}) collective-permute-start(bf16[1,4,128,256]{3,2,1,0:T(8,128)(2,1)S(1)} %fusion.66), channel_id=1, source_target_pairs={{8,0},{16,8},{24,16},{9,1},{17,9},{25,17},{10,2},{18,10},{26,18},{... | collective-permute-start | bytes 786440 | tf_op jit(solution)/shard_map/ppermute | solution.py:20
  49.3 9.0 %collective-permute-start.6 = (bf16[3,1,128,256]{3,2,1,0:T(8,128)(2,1)}, bf16[3,1,128,256]{3,2,1,0:T(8,128)(2,1)}, u32[]{:S(2)}, u32[]{:S(2)}) collective-permute-start(bf16[3,1,128,256]{3,2,1,0:T(8,128)(2,1)} %get-tuple-element.248), channel_id=1, source_target_pairs={{0,1},{1,2},{2,3},{3,4},{4,5},{5,6},{6,7},{8,9},{9,10},{10,11},{11... | collective-permute-start | bytes 589832 | tf_op jit(solution)/shard_map/ppermute | solution.py:18
  54.6 5.0 %collective-permute-start.7 = (bf16[3,1,128,256]{3,2,1,0:T(8,128)(2,1)}, bf16[3,1,128,256]{3,2,1,0:T(8,128)(2,1)S(1)}, u32[]{:S(2)}, u32[]{:S(2)}) collective-permute-start(bf16[3,1,128,256]{3,2,1,0:T(8,128)(2,1)} %get-tuple-element.247), channel_id=1, source_target_pairs={{1,0},{2,1},{3,2},{4,3},{5,4},{6,5},{7,6},{9,8},{10,9},{11,10},{12... | collective-permute-start | bytes 589832 | tf_op jit(solution)/shard_map/ppermute | solution.py:20
  59.7 2.4 copy-start.12
  62.1 1.1 copy-start.10
  63.3 1.0 copy-start.9
  63.6 1.0 copy-start.13
  64.6 1.0 copy-start.8
  64.9 1.1 copy-start.7
  66.0 1.0 copy-start.14
  66.0 1.1 copy-start.25
  66.4 1.0 copy-start.6
  67.5 1.0 copy-start.5
  68.5 1.0 copy-start.4
  68.8 1.0 copy-start.18
  70.9 2.7 copy-start.15
  70.9 2.7 copy-start.19
  70.9 17.9 %copy-start.16 = (f32[2048]{0:T(1024)S(1)}, f32[2048]{0:T(1024)}, u32[]{:S(2)}) copy-start(f32[2048]{0:T(1024)} %param.24) | copy-start | bytes 24580
  90.2 1.3 copy-start.20
  90.2 1.5 copy-start.21
  90.2 1.8 copy-start.22
  90.2 1.8 copy-start.23
  96.4 14.2 %collective-permute-start.8 = (bf16[1024,256]{0,1:T(8,128)(2,1)S(1)}, bf16[1024,256]{0,1:T(8,128)(2,1)S(1)}, u32[]{:S(2)}, u32[]{:S(2)}) collective-permute-start(bf16[1024,256]{0,1:T(8,128)(2,1)S(1)} %get-tuple-element.197), channel_id=1, source_target_pairs={{0,24},{8,0},{16,8},{24,16},{1,25},{9,1},{17,9},{25,17},{2,26},{10... | collective-permute-start | bytes 1572872 | tf_op jit(solution)/shard_map/ppermute | solution.py:79
  110.8 48.0 %collective-permute-start.9 = (bf16[2048,256]{0,1:T(8,128)(2,1)S(1)}, bf16[2048,256]{0,1:T(8,128)(2,1)S(1)}, u32[]{:S(2)}, u32[]{:S(2)}) collective-permute-start(bf16[2048,256]{0,1:T(8,128)(2,1)S(1)} %pad_maximum_fusion), channel_id=1, source_target_pairs={{0,16},{8,24},{16,0},{24,8},{1,17},{9,25},{17,1},{25,9},{2,18},{10... | collective-permute-start | bytes 3145736 | tf_op jit(solution)/shard_map/ppermute | solution.py:79
  159.8 2.0 copy-start.3
  161.7 180.8 %reduce-scatter.2.cloned.1.call-start = ((), (), s32[]{:S(2)}) async-start(), calls=%async_computation.2 | async-start | bytes 294912 | tf_op jit(solution)/shard_map/reduce_scatter | solution.py:147
  308.0 0.8 copy-start.17
  308.0 36.0 %copy-start.1 = (bf16[128,2048]{1,0:T(8,128)(2,1)S(1)}, bf16[128,2048]{1,0:T(8,128)(2,1)}, u32[]{:S(2)}) copy-start(bf16[128,2048]{1,0:T(8,128)(2,1)} %param.23) | copy-start | bytes 1572868
Sparse Core Ops, SparseCore 0:
  161.9 44.4 all-gather.1
  310.0 32.4 reduce-scatter.1
